TPU v7x, 32 devices: a whole 2x2x4 slice. The times are simulated.
32 devices in a mesh: seq: 16 (over z, x, core), ch: 2 (over y).
Axes of the slice: x: 2, y: 2, z: 4, core: 2. Of those that a mesh axis runs over, the one named last changes fastest.
Arguments:
- projected: float32 [3, 32, 16, 2048], P(None, None, 'seq', 'ch'), may hold values from -6 to 6
- filter_taps: float32 [32, 16, 2048], P('ch', 'seq'), may hold values from -1.1 to 1.1
- skip_gain: float32 [32], P('ch'), may hold values from -4 to 4
Outputs:
- mixed: float32 [32, 16, 2048], P('ch', 'seq')
All inputs are finite; a program needn't handle non-finite values.
Results may differ from a plain program's by a relative error of at most 0.00013.
Values sent between devices are 32-bit elements; how exact they have to be, the bound alone decides.
A program may use at most 64 MiB of HBM per device.

v0:
```python
from functools import partial
import math

import jax
import jax.numpy as jnp
from jax import lax
from jax.sharding import PartitionSpec as P


def partner_2(value, axis, distance):
    mask = 2**distance
    pairs = [(source, source ^ mask) for source in range(lax.axis_size(axis))]
    return lax.ppermute(value, axis, pairs)


def phase_of(sign, numer, denom):
    angle = sign * 2.0 * math.pi / denom * (numer % denom).astype(jnp.float32)
    return (jnp.cos(angle), jnp.sin(angle))


def rotate(blocks, cosine, sine_part):
    real_part = blocks[0]
    imag_part = blocks[1]
    return jnp.stack(
        [real_part * cosine - imag_part * sine_part, real_part * sine_part + imag_part * cosine]
    )


def complex_times(left, right):
    return jnp.stack(
        [left[0] * right[0] - left[1] * right[1], left[0] * right[1] + left[1] * right[0]]
    )


def dft_matrix(order, sign):
    counter = jnp.arange(order, dtype=jnp.int32)
    return phase_of(sign, counter[:, None] * counter[None, :], order)


def complex_einsum(form, blocks, cosine, sine_part):
    product = partial(jnp.einsum, precision=lax.Precision.HIGHEST)
    real_part = product(form, blocks[0], cosine) - product(form, blocks[1], sine_part)
    imag_part = product(form, blocks[0], sine_part) + product(form, blocks[1], cosine)
    return jnp.stack([real_part, imag_part])


def factor_pair(length):
    second = math.gcd(length, 128)
    return (length // second, second)


def slot_frequency(length):
    first, second = factor_pair(length)
    slot = jnp.arange(length, dtype=jnp.int32)
    return slot // second + first * (slot % second)


def local_forward(blocks):
    batch = blocks.shape[1]
    length = blocks.shape[2]
    first, second = factor_pair(length)
    shaped = blocks.reshape(2, batch, first, second)
    cosine, sine_part = dft_matrix(first, -1)
    shaped = complex_einsum("bjk,jm->bmk", shaped, cosine, sine_part)
    outer_index = jnp.arange(first, dtype=jnp.int32)[:, None]
    inner_index = jnp.arange(second, dtype=jnp.int32)[None, :]
    cosine, sine_part = phase_of(-1, outer_index * inner_index, length)
    shaped = rotate(shaped, cosine, sine_part)
    cosine, sine_part = dft_matrix(second, -1)
    shaped = complex_einsum("bmk,kn->bmn", shaped, cosine, sine_part)
    return shaped.reshape(2, batch, length)


def local_inverse(blocks):
    batch = blocks.shape[1]
    length = blocks.shape[2]
    first, second = factor_pair(length)
    shaped = blocks.reshape(2, batch, first, second)
    cosine, sine_part = dft_matrix(second, 1)
    shaped = complex_einsum("bmn,nk->bmk", shaped, cosine, sine_part)
    outer_index = jnp.arange(first, dtype=jnp.int32)[:, None]
    inner_index = jnp.arange(second, dtype=jnp.int32)[None, :]
    cosine, sine_part = phase_of(1, outer_index * inner_index, length)
    shaped = rotate(shaped, cosine, sine_part)
    cosine, sine_part = dft_matrix(first, 1)
    shaped = complex_einsum("bmk,mj->bjk", shaped, cosine, sine_part)
    return shaped.reshape(2, batch, length)


def swaps_forward(blocks):
    shards = lax.axis_size("seq")
    position = lax.axis_index("seq")
    levels = shards.bit_length() - 1
    for level in reversed(range(levels)):
        stride = 1 << level
        partner = partner_2(blocks, "seq", level)
        is_upper = position // stride % 2 == 1
        cosine, sine_part = phase_of(-1, position % stride * (shards // (2 * stride)), shards)
        upper_value = rotate(partner - blocks, cosine, sine_part)
        blocks = jnp.where(is_upper, upper_value, blocks + partner)
    return blocks


def swaps_inverse(blocks):
    shards = lax.axis_size("seq")
    position = lax.axis_index("seq")
    levels = shards.bit_length() - 1
    for level in range(levels):
        stride = 1 << level
        partner = partner_2(blocks, "seq", level)
        is_upper = position // stride % 2 == 1
        cosine, sine_part = phase_of(1, position % stride * (shards // (2 * stride)), shards)
        lower_value = blocks + rotate(partner, cosine, sine_part)
        upper_value = partner - rotate(blocks, cosine, sine_part)
        blocks = jnp.where(is_upper, upper_value, lower_value)
    return blocks


def on_device(projected, filter_taps, skip_gain):
    arrived = lax.all_to_all(projected, "ch", split_axis=1, concat_axis=3, tiled=True)
    value_row = arrived[0][:, 0]
    inner_gate = arrived[1][:, 0]
    outer_gate = arrived[2][:, 0]
    gated = inner_gate * value_row
    channels = gated.shape[0]
    length = gated.shape[1]
    shards = lax.axis_size("seq")
    position = lax.axis_index("seq")
    real_rows = jnp.concatenate([gated, filter_taps[:, 0]], axis=0)
    moment = position + shards * jnp.arange(length, dtype=jnp.int32)
    cosine, sine_part = phase_of(-1, moment, 2 * shards * length)
    real_part = jnp.concatenate([real_rows, real_rows * cosine], axis=0)
    imag_part = jnp.concatenate([jnp.zeros_like(real_rows), real_rows * sine_part], axis=0)
    blocks = local_forward(jnp.stack([real_part, imag_part]))
    frequency = slot_frequency(length)
    cosine, sine_part = phase_of(-1, position * frequency, shards * length)
    blocks = rotate(blocks, cosine, sine_part)
    spectrum = swaps_forward(blocks)
    gated_even = spectrum[:, :channels]
    filter_even = spectrum[:, channels : 2 * channels]
    gated_odd = spectrum[:, 2 * channels : 3 * channels]
    filter_odd = spectrum[:, 3 * channels :]
    product = jnp.concatenate(
        [complex_times(gated_even, filter_even), complex_times(gated_odd, filter_odd)], axis=1
    )
    signal = swaps_inverse(product)
    cosine, sine_part = phase_of(1, position * frequency, shards * length)
    signal = local_inverse(rotate(signal, cosine, sine_part))
    cosine, sine_part = phase_of(1, moment, 2 * shards * length)
    even_part = signal[:, :channels]
    odd_part = signal[:, channels:]
    summed = even_part[0] + cosine * odd_part[0] - sine_part * odd_part[1]
    conv = summed * (1.0 / (2 * shards * length))
    result = outer_gate * (conv + skip_gain[:, None] * gated)
    return result[:, None, :]


def solution(mesh):
    return jax.shard_map(
        on_device,
        mesh=mesh,
        in_specs=(P(None, None, "seq", "ch"), P("ch", "seq", None), P("ch")),
        out_specs=P("ch", "seq", None),
        check_vma=False,
    )
```

profile of v0, /device:TPU:0, one launch (start us, length us, event | category | flops | bytes accessed | tf_op | source)
XLA Modules:
  0.0 187.9 jit_solution(9763778947393743644)
XLA Ops:
  0.0 1.8 copy.19
  1.8 4.4 %all-to-all-start = ((f32[3,32,1,1024]{3,2,0,1:T(1,128)}), f32[3,32,1,1024]{3,2,0,1:T(1,128)S(1)}, u32[]{:S(2)}, u32[]{:S(2)}) async-start(f32[3,32,1,1024]{3,2,0,1:T(1,128)} %copy.19), calls=%async_computation | async-start | bytes 786432 | tf_op jit(solution)/shard_map/all_to_all | solution.py:120
  6.6 6.8 %all-to-all-done = f32[3,32,1,1024]{3,2,0,1:T(1,128)S(1)} async-done(((f32[3,32,1,1024]{3,2,0,1:T(1,128)}), f32[3,32,1,1024]{3,2,0,1:T(1,128)S(1)}, u32[]{:S(2)}, u32[]{:S(2)}) %all-to-all-start) | async-done | bytes 393248 | tf_op jit(solution)/shard_map/all_to_all | solution.py:120
  16.5 0.8 fusion.8
  17.4 0.8 fusion.10
  18.2 0.8 convolution_add_fusion
  19.1 0.8 convolution_subtract_fusion
  20.3 2.9 %collective-permute-start = (f32[2,64,2048]{2,1,0:T(8,128)S(1)}, f32[2,64,2048]{2,1,0:T(8,128)S(1)}, u32[]{:S(2)}, u32[]{:S(2)}) collective-permute-start(f32[2,64,2048]{2,1,0:T(8,128)S(1)} %pad_maximum_fusion), channel_id=1, source_target_pairs={{0,16},{2,18},{4,20},{6,22},{8,24},{10,26},{12,28},{14,30},{16,0},... | collective-permute-start | bytes 3145736 | tf_op jit(solution)/shard_map/ppermute | solution.py:13
  23.4 44.7 %collective-permute-done = f32[2,64,2048]{2,1,0:T(8,128)S(1)} collective-permute-done((f32[2,64,2048]{2,1,0:T(8,128)S(1)}, f32[2,64,2048]{2,1,0:T(8,128)S(1)}, u32[]{:S(2)}, u32[]{:S(2)}) %collective-permute-start) | collective-permute-done | bytes 1048608 | tf_op jit(solution)/shard_map/ppermute | solution.py:13
  68.3 1.3 maximum_select_fusion
  70.4 23.6 %collective-permute-done.1 = f32[2,64,2048]{2,1,0:T(8,128)} collective-permute-done((f32[2,64,2048]{2,1,0:T(8,128)}, f32[2,64,2048]{2,1,0:T(8,128)}, u32[]{:S(2)}, u32[]{:S(2)}) %collective-permute-start.1) | collective-permute-done | bytes 1048608 | tf_op jit(solution)/shard_map/ppermute | solution.py:13
  94.1 1.5 fusion.197
  95.7 0.9 copy-done.1
  96.8 1.6 maximum_select_fusion.1
  98.4 1.4 collective-permute-start.2
  100.0 21.8 %collective-permute-done.2 = f32[2,64,2048]{2,1,0:T(8,128)S(1)} collective-permute-done((f32[2,64,2048]{2,1,0:T(8,128)S(1)}, f32[2,64,2048]{2,1,0:T(8,128)S(1)}, u32[]{:S(2)}, u32[]{:S(2)}) %collective-permute-start.2) | collective-permute-done | bytes 1048608 | tf_op jit(solution)/shard_map/ppermute | solution.py:13
  122.4 2.6 %collective-permute-done.3 = f32[2,64,2048]{2,1,0:T(8,128)S(1)} collective-permute-done((f32[2,64,2048]{2,1,0:T(8,128)S(1)}, f32[2,64,2048]{2,1,0:T(8,128)S(1)}, u32[]{:S(2)}, u32[]{:S(2)}) %collective-permute-start.3) | collective-permute-done | bytes 1048608 | tf_op jit(solution)/shard_map/ppermute | solution.py:13
  125.8 1.7 collective-permute-done.4
  127.7 1.6 collective-permute-start.5
  129.7 12.1 %collective-permute-done.5 = f32[2,32,2048]{2,1,0:T(8,128)S(1)} collective-permute-done((f32[2,32,2048]{2,1,0:T(8,128)S(1)}, f32[2,32,2048]{2,1,0:T(8,128)S(1)}, u32[]{:S(2)}, u32[]{:S(2)}) %collective-permute-start.5) | collective-permute-done | bytes 524320 | tf_op jit(solution)/shard_map/ppermute | solution.py:13
  142.1 2.5 %collective-permute-start.6 = (f32[2,32,2048]{2,1,0:T(8,128)S(1)}, f32[2,32,2048]{2,1,0:T(8,128)S(1)}, u32[]{:S(2)}, u32[]{:S(2)}) collective-permute-start(f32[2,32,2048]{2,1,0:T(8,128)S(1)} %fusion.3), channel_id=1, source_target_pairs={{0,8},{2,10},{4,12},{6,14},{8,0},{10,2},{12,4},{14,6},{16,24},{18,... | collective-permute-start | bytes 1572872 | tf_op jit(solution)/shard_map/ppermute | solution.py:13
  144.8 11.2 %collective-permute-done.6 = f32[2,32,2048]{2,1,0:T(8,128)S(1)} collective-permute-done((f32[2,32,2048]{2,1,0:T(8,128)S(1)}, f32[2,32,2048]{2,1,0:T(8,128)S(1)}, u32[]{:S(2)}, u32[]{:S(2)}) %collective-permute-start.6) | collective-permute-done | bytes 524320 | tf_op jit(solution)/shard_map/ppermute | solution.py:13
  156.2 3.7 %collective-permute-start.7 = (f32[2,32,2048]{2,1,0:T(8,128)S(1)}, f32[2,32,2048]{2,1,0:T(8,128)S(1)}, u32[]{:S(2)}, u32[]{:S(2)}) collective-permute-start(f32[2,32,2048]{2,1,0:T(8,128)S(1)} %fusion.4), channel_id=1, source_target_pairs={{0,16},{2,18},{4,20},{6,22},{8,24},{10,26},{12,28},{14,30},{16,0},... | collective-permute-start | bytes 1572872 | tf_op jit(solution)/shard_map/ppermute | solution.py:13
  160.8 20.9 %collective-permute-done.7 = f32[2,32,2048]{2,1,0:T(8,128)S(1)} collective-permute-done((f32[2,32,2048]{2,1,0:T(8,128)S(1)}, f32[2,32,2048]{2,1,0:T(8,128)S(1)}, u32[]{:S(2)}, u32[]{:S(2)}) %collective-permute-start.7) | collective-permute-done | bytes 524320 | tf_op jit(solution)/shard_map/ppermute | solution.py:13
  (81 shorter events, 13.9 us)
Async XLA Ops:
  1.8 4.6 %copy-start.4 = (f32[16,1,2048]{2,1,0:T(1,128)S(1)}, f32[16,1,2048]{2,1,0:T(1,128)}, u32[]{:S(2)}) copy-start(f32[16,1,2048]{2,1,0:T(1,128)} %param.4) | copy-start | bytes 393220
  1.8 11.7 %all-to-all-start = ((f32[3,32,1,1024]{3,2,0,1:T(1,128)}), f32[3,32,1,1024]{3,2,0,1:T(1,128)S(1)}, u32[]{:S(2)}, u32[]{:S(2)}) async-start(f32[3,32,1,1024]{3,2,0,1:T(1,128)} %copy.19), calls=%async_computation | async-start | bytes 786432 | tf_op jit(solution)/shard_map/all_to_all | solution.py:120
  20.3 47.8 %collective-permute-start = (f32[2,64,2048]{2,1,0:T(8,128)S(1)}, f32[2,64,2048]{2,1,0:T(8,128)S(1)}, u32[]{:S(2)}, u32[]{:S(2)}) collective-permute-start(f32[2,64,2048]{2,1,0:T(8,128)S(1)} %pad_maximum_fusion), channel_id=1, source_target_pairs={{0,16},{2,18},{4,20},{6,22},{8,24},{10,26},{12,28},{14,30},{16,0},... | collective-permute-start | bytes 3145736 | tf_op jit(solution)/shard_map/ppermute | solution.py:13
  68.3 25.7 %copy-start = (f32[1,64,2048]{2,1,0:T(8,128)}, f32[1,64,2048]{2,1,0:T(8,128)S(1)}, u32[]{:S(2)}) copy-start(f32[1,64,2048]{2,1,0:T(8,128)S(1)} %get-tuple-element.17) | copy-start | bytes 1572868
  68.3 25.7 %copy-start.2 = (f32[1,64,2048]{2,1,0:T(8,128)}, f32[1,64,2048]{2,1,0:T(8,128)S(1)}, u32[]{:S(2)}) copy-start(f32[1,64,2048]{2,1,0:T(8,128)S(1)} %get-tuple-element.18) | copy-start | bytes 1572868
  69.6 24.4 %collective-permute-start.1 = (f32[2,64,2048]{2,1,0:T(8,128)}, f32[2,64,2048]{2,1,0:T(8,128)}, u32[]{:S(2)}, u32[]{:S(2)}) collective-permute-start(f32[2,64,2048]{2,1,0:T(8,128)} %maximum_select_fusion), channel_id=1, source_target_pairs={{0,8},{2,10},{4,12},{6,14},{8,0},{10,2},{12,4},{14,6},{16,24},{18,... | collective-permute-start | bytes 3145736 | tf_op jit(solution)/shard_map/ppermute | solution.py:13
  95.6 1.0 copy-start.1
  95.6 1.2 copy-start.3
  98.4 23.4 %collective-permute-start.2 = (f32[2,64,2048]{2,1,0:T(8,128)S(1)}, f32[2,64,2048]{2,1,0:T(8,128)S(1)}, u32[]{:S(2)}, u32[]{:S(2)}) collective-permute-start(f32[2,64,2048]{2,1,0:T(8,128)S(1)} %maximum_select_fusion.1), channel_id=1, source_target_pairs={{0,4},{2,6},{4,0},{6,2},{8,12},{10,14},{12,8},{14,10},{16,20},{18,... | collective-permute-start | bytes 3145736 | tf_op jit(solution)/shard_map/ppermute | solution.py:13
  122.3 2.7 %collective-permute-start.3 = (f32[2,64,2048]{2,1,0:T(8,128)S(1)}, f32[2,64,2048]{2,1,0:T(8,128)S(1)}, u32[]{:S(2)}, u32[]{:S(2)}) collective-permute-start(f32[2,64,2048]{2,1,0:T(8,128)S(1)} %maximum_select_fusion.2), channel_id=1, source_target_pairs={{0,2},{2,0},{4,6},{6,4},{8,10},{10,8},{12,14},{14,12},{16,18},{18,... | collective-permute-start | bytes 3145736 | tf_op jit(solution)/shard_map/ppermute | solution.py:13
  125.6 2.0 %collective-permute-start.4 = (f32[2,32,2048]{2,1,0:T(8,128)S(1)}, f32[2,32,2048]{2,1,0:T(8,128)S(1)}, u32[]{:S(2)}, u32[]{:S(2)}) collective-permute-start(f32[2,32,2048]{2,1,0:T(8,128)S(1)} %maximum_maximum_fusion), channel_id=1, source_target_pairs={{0,2},{2,0},{4,6},{6,4},{8,10},{10,8},{12,14},{14,12},{16,18},{18,... | collective-permute-start | bytes 1572872 | tf_op jit(solution)/shard_map/ppermute | solution.py:13
  127.7 14.0 %collective-permute-start.5 = (f32[2,32,2048]{2,1,0:T(8,128)S(1)}, f32[2,32,2048]{2,1,0:T(8,128)S(1)}, u32[]{:S(2)}, u32[]{:S(2)}) collective-permute-start(f32[2,32,2048]{2,1,0:T(8,128)S(1)} %fusion.2), channel_id=1, source_target_pairs={{0,4},{2,6},{4,0},{6,2},{8,12},{10,14},{12,8},{14,10},{16,20},{18,... | collective-permute-start | bytes 1572872 | tf_op jit(solution)/shard_map/ppermute | solution.py:13
  142.1 13.9 %collective-permute-start.6 = (f32[2,32,2048]{2,1,0:T(8,128)S(1)}, f32[2,32,2048]{2,1,0:T(8,128)S(1)}, u32[]{:S(2)}, u32[]{:S(2)}) collective-permute-start(f32[2,32,2048]{2,1,0:T(8,128)S(1)} %fusion.3), channel_id=1, source_target_pairs={{0,8},{2,10},{4,12},{6,14},{8,0},{10,2},{12,4},{14,6},{16,24},{18,... | collective-permute-start | bytes 1572872 | tf_op jit(solution)/shard_map/ppermute | solution.py:13
  156.2 25.5 %collective-permute-start.7 = (f32[2,32,2048]{2,1,0:T(8,128)S(1)}, f32[2,32,2048]{2,1,0:T(8,128)S(1)}, u32[]{:S(2)}, u32[]{:S(2)}) collective-permute-start(f32[2,32,2048]{2,1,0:T(8,128)S(1)} %fusion.4), channel_id=1, source_target_pairs={{0,16},{2,18},{4,20},{6,22},{8,24},{10,26},{12,28},{14,30},{16,0},... | collective-permute-start | bytes 1572872 | tf_op jit(solution)/shard_map/ppermute | solution.py:13
  186.4 0.7 copy-start.5
where the time goes:
time: 188 us
  waiting for transfers between devices  146 us (78%)
  starting transfers between devices  17.4 us (9%)
  matrix products  9.85 us (5%)
  other arithmetic  7.85 us (4%)
  local copies, waits for them, and re-layouts  5.68 us (3%)
    ppermute x8, waiting for transfers between devices, partner_2(): return lax.ppermute(value, axis, pairs)  139 us
    ppermute x8, starting transfers between devices, partner_2(): return lax.ppermute(value, axis, pairs)  13 us
    all_to_all x1, waiting for transfers between devices, on_device(): lax.all_to_all(projected, 'ch', split_axis=1, concat_axis=3, tiled=True)  6.84 us
    all_to_all x1, starting transfers between devices, on_device(): lax.all_to_all(projected, 'ch', split_axis=1, concat_axis=3, tiled=True)  4.39 us
    unnamed x20, local copies, waits for them, and re-layouts  3.83 us
  transfers between devices with their start and end apart: 9, of which 9 were waited for; matrix products, arithmetic and copies ran while one was open for 1% of the time, Pallas kernels for 0%

commit v1 on v0

v1 whole, which is shorter than its diff:
```python
import functools

import jax
import jax.numpy as jnp
import numpy as np
from jax import lax
from jax.experimental import pallas as pl
from jax.experimental.pallas import tpu as pltpu
from jax.sharding import PartitionSpec as P

MESH = pl.DeviceIdType.MESH
LANES = 128
ROWS = 256


def split_np(table):
    high = table.astype(np.float32).astype(jnp.bfloat16)
    low = (table - high.astype(np.float64)).astype(np.float32).astype(jnp.bfloat16)
    return np.stack([high, low])


def tables(shards, tiles):
    order = 2 * tiles
    length = shards * LANES * order
    per_group = ROWS // tiles
    keys = LANES // shards
    ka = np.arange(tiles) + 0.5
    a = np.arange(tiles)
    angle = 2 * np.pi * np.outer(ka, a) / order
    eye = np.eye(per_group)
    first = np.concatenate(
        [
            np.einsum("ka,pq->kpqa", part, eye).reshape(tiles * per_group, ROWS)
            for part in (np.cos(angle), -np.sin(angle))
        ]
    )
    last = first.T * (2.0 / length)
    b = np.arange(LANES)
    angle = 2 * np.pi * (np.outer(b, b) % LANES) / LANES
    cosine, sine = np.cos(angle), np.sin(angle)
    lane = np.block([[cosine, -sine], [sine, cosine]])
    p = np.arange(shards)
    angle = 2 * np.pi * (np.outer(p, p) % shards) / shards
    cosine, sine = np.kron(np.eye(keys), np.cos(angle)), np.kron(np.eye(keys), np.sin(angle))
    shard = np.block([[cosine, sine], [-sine, cosine]])
    low = (p[:, None] + shards * b[None, :])[None]
    angle = -2 * np.pi * ka[:, None, None] * low / length
    angle = angle.reshape(tiles * shards, LANES)
    turn_one = np.stack([np.cos(angle), np.sin(angle)]).astype(np.float32)
    angle = -2 * np.pi * np.outer(p, b) / (LANES * shards)
    angle = np.tile(angle, (keys, 1))
    turn_two = np.stack([np.cos(angle), np.sin(angle)]).astype(np.float32)
    return (
        split_np(first),
        split_np(last),
        split_np(lane),
        split_np(shard),
        turn_one,
        turn_two,
    )


def parts_of(x):
    high = x.astype(jnp.bfloat16)
    low = (x - high.astype(jnp.float32)).astype(jnp.bfloat16)
    return high, low


def dot(left, right):
    return jnp.dot(left, right, preferred_element_type=jnp.float32)


def from_left(table, x):
    high, low = parts_of(x)
    return dot(table[0], high) + (dot(table[0], low) + dot(table[1], high))


def from_left_narrow(table, x):
    high, low = parts_of(x)
    both = dot(table[0], jnp.concatenate([high, low], axis=1))
    width = x.shape[1]
    return both[:, :width] + (both[:, width:] + dot(table[1], high))


def from_right(x, table):
    high, low = parts_of(x)
    return dot(high, table[0]) + (dot(low, table[0]) + dot(high, table[1]))


def convolve(gated, taps, shards, tiles, first, last, lane, shard, turn_one, turn_two):
    per_group = ROWS // tiles
    groups = shards // per_group
    rows = tiles * shards
    stages = []
    for g in range(groups):
        chosen = slice(g * ROWS, (g + 1) * ROWS)
        both = jnp.concatenate([gated[chosen], taps[chosen]], axis=1)
        stages.append(from_left(first, both))

    def rows_of(part, signal):
        pieces = [
            s[part * ROWS : (part + 1) * ROWS, signal * LANES : (signal + 1) * LANES] for s in stages
        ]
        if groups == 1:
            return pieces[0]
        pieces = [x.reshape(tiles, per_group, LANES) for x in pieces]
        return jnp.concatenate(pieces, axis=1).reshape(rows, LANES)

    one_re, one_im = turn_one[0], turn_one[1]
    two_re, two_im = turn_two[0], turn_two[1]
    spectra = []
    for signal in range(2):
        re, im = rows_of(0, signal), rows_of(1, signal)
        turned = jnp.concatenate([re * one_re - im * one_im, re * one_im + im * one_re], axis=1)
        spectra.append(from_right(turned, lane))
    backs = []
    for q in range(rows // LANES):
        chosen = slice(q * LANES, (q + 1) * LANES)
        res, ims = [], []
        for signal in range(2):
            re, im = spectra[signal][chosen, :LANES], spectra[signal][chosen, LANES:]
            res.append(re * two_re - im * two_im)
            ims.append(re * two_im + im * two_re)
        stacked = jnp.concatenate(
            [jnp.concatenate(res, axis=1), jnp.concatenate(ims, axis=1)], axis=0
        )
        full = from_left(shard, stacked)
        g_re, h_re = full[:LANES, :LANES], full[:LANES, LANES:]
        g_im, h_im = full[LANES:, :LANES], full[LANES:, LANES:]
        y_re = g_re * h_re - g_im * h_im
        y_im = g_re * h_im + g_im * h_re
        backs.append(jnp.concatenate([y_im, y_re], axis=0))
    turned = []
    for q in range(0, len(backs), 2):
        back = from_left(shard, jnp.concatenate(backs[q : q + 2], axis=1))
        for half in range(2):
            columns = slice(half * LANES, (half + 1) * LANES)
            re, im = back[LANES:, columns], back[:LANES, columns]
            turned.append(
                jnp.concatenate([im * two_re - re * two_im, re * two_re + im * two_im], axis=1)
            )
    back = from_right(jnp.concatenate(turned, axis=0), lane)
    re, im = back[:, LANES:], back[:, :LANES]
    out_re = re * one_re + im * one_im
    out_im = im * one_re - re * one_im
    results = []
    for g in range(groups):
        if groups == 1:
            stacked = jnp.concatenate([out_re, out_im], axis=0)
        else:
            part = slice(g * per_group, (g + 1) * per_group)
            stacked = jnp.concatenate(
                [
                    x.reshape(tiles, shards, LANES)[:, part].reshape(ROWS, LANES)
                    for x in (out_re, out_im)
                ],
                axis=0,
            )
        results.append(from_left_narrow(last, stacked))
    return results[0] if groups == 1 else jnp.concatenate(results, axis=0)


def far_first(count):
    return sorted(range(1, count), key=lambda d: (-min(d, count - d), d))


def kernel(
    shards, copies, channels, tiles,
    projected, taps, gain, *rest,
):
    table_refs, rest = rest[:6], rest[6:]
    out, rest = rest[0], rest[1:]
    held, rest = rest[:6], rest[6:]
    (
        inner, sending, g_in, h_in, outer, conv, y_in, gain_in,
        load_sem, table_sem, g_send, g_recv, h_send, h_recv, o_send, o_recv, y_send, y_recv,
    ) = rest
    me = lax.axis_index("seq")
    mine = lax.axis_index("ch")
    stride = shards // channels
    total = shards * copies
    rank = me * copies + mine

    barrier = pltpu.get_barrier_semaphore()
    for d in far_first(total):
        other = (rank + d) % total
        pl.semaphore_signal(
            barrier,
            inc=1,
            device_id={"seq": other // copies, "ch": other % copies},
            device_id_type=MESH,
        )
    load = pltpu.make_async_copy(projected.at[pl.ds(0, 2)], inner, load_sem.at[0])
    load.start()
    load_gain = pltpu.make_async_copy(gain, gain_in, load_sem.at[1])
    load_gain.start()
    loads = [
        pltpu.make_async_copy(table_refs[i], held[i], table_sem.at[i]) for i in range(6)
    ]
    for x in loads:
        x.start()
    load.wait()
    sending[...] = inner[0] * inner[1]
    pl.semaphore_wait(barrier, total - 1)

    owners = channels * copies
    own_slot = me // stride

    def send_gated(owner):
        index, target = owner // copies, owner % copies
        pltpu.make_async_remote_copy(
            src_ref=sending.at[target * channels + index],
            dst_ref=g_in.at[me, mine],
            send_sem=g_send,
            recv_sem=g_recv,
            device_id={"seq": index * stride, "ch": target},
            device_id_type=MESH,
        ).start()

    def send_taps(index):
        pltpu.make_async_remote_copy(
            src_ref=taps.at[index],
            dst_ref=h_in.at[me],
            send_sem=h_send,
            recv_sem=h_recv,
            device_id={"seq": index * stride, "ch": mine},
            device_id_type=MESH,
        ).start()

    is_owner = me % stride == 0
    own_channel = mine * channels + own_slot

    def when_owner(body):
        if stride == 1:
            body()
        else:
            pl.when(is_owner)(body)

    def when_not_owner(body):
        if stride > 1:
            pl.when(jnp.logical_not(is_owner))(body)

    for d in far_first(channels):
        send_taps((own_slot + d) % channels)
    own_rank = own_slot * copies + mine
    for d in far_first(owners):
        send_gated((own_rank + d) % owners)
    when_not_owner(lambda: send_gated(own_rank))
    when_not_owner(lambda: send_taps(own_slot))
    for d in range(1, copies):
        target = (mine + d) % copies
        pltpu.make_async_remote_copy(
            src_ref=projected.at[2, pl.ds(target * channels, channels)],
            dst_ref=outer.at[mine],
            send_sem=o_send,
            recv_sem=o_recv,
            device_id={"seq": me, "ch": target},
            device_id_type=MESH,
        ).start()
    pltpu.make_async_copy(
        projected.at[2, pl.ds(mine * channels, channels)], outer.at[mine], o_recv
    ).start()

    def own_blocks():
        pltpu.make_async_copy(sending.at[own_channel], g_in.at[me, mine], g_recv).start()
        pltpu.make_async_copy(taps.at[own_slot], h_in.at[me], h_recv).start()

    when_owner(own_blocks)
    load_gain.wait()
    for x in loads:
        x.wait()

    def transform():
        pltpu.make_async_copy(h_in, h_in, h_recv).wait()
        pltpu.make_async_copy(g_in, g_in, g_recv).wait()
        slab = gain_in[...]
        column = lax.broadcasted_iota(jnp.int32, slab.shape, 1)
        direct = jnp.sum(jnp.where(column == own_slot, slab, 0.0))
        signal = g_in[...].reshape(shards * tiles, LANES)
        filt = h_in[...].reshape(shards * tiles, LANES)
        row = lax.broadcasted_iota(jnp.int32, filt.shape, 0)
        column = lax.broadcasted_iota(jnp.int32, filt.shape, 1)
        filt = filt + jnp.where((row == 0) & (column == 0), direct, 0.0)
        result = convolve(signal, filt, shards, tiles, *held)
        conv[...] = result.reshape(shards, tiles, LANES)
        for d in far_first(shards):
            target = (me + d) % shards
            pltpu.make_async_remote_copy(
                src_ref=conv.at[target],
                dst_ref=y_in.at[own_slot],
                send_sem=y_send,
                recv_sem=y_recv,
                device_id={"seq": target, "ch": mine},
                device_id_type=MESH,
            ).start()
        pltpu.make_async_copy(conv.at[me], y_in.at[own_slot], y_recv).start()

    when_owner(transform)
    pltpu.make_async_copy(outer, outer, o_recv).wait()
    pltpu.make_async_copy(y_in, y_in, y_recv).wait()
    step = tiles // copies
    for c in range(copies):
        part = slice(c * step, (c + 1) * step)
        out[:, part] = y_in[:, part] * outer[c]

    def sent(ref, sem):
        pltpu.make_async_copy(ref, ref, sem).wait()

    def sent_by_owner():
        sent(conv.at[pl.ds(0, shards - 1)], y_send)
        sent(sending.at[pl.ds(0, owners - 1)], g_send)
        if channels > 1:
            sent(h_in.at[pl.ds(0, channels - 1)], h_send)

    def sent_by_other():
        sent(sending.at[pl.ds(0, owners)], g_send)
        sent(h_in.at[pl.ds(0, channels)], h_send)

    when_owner(sent_by_owner)
    when_not_owner(sent_by_other)
    if copies > 1:
        sent(outer.at[pl.ds(0, copies - 1)], o_send)


def on_device(shards, copies, projected, filter_taps, skip_gain):
    _, all_channels, _, part = projected.shape
    channels, _, length = filter_taps.shape
    tiles = length // LANES
    step = part // LANES
    constants = [jnp.asarray(x) for x in tables(shards, tiles)]
    any_spec = pl.BlockSpec(memory_space=pl.ANY)
    f32 = jnp.float32
    result = pl.pallas_call(
        functools.partial(kernel, shards, copies, channels, tiles),
        out_shape=jax.ShapeDtypeStruct((channels, tiles, LANES), f32),
        in_specs=[any_spec] * 9,
        out_specs=pl.BlockSpec(memory_space=pltpu.VMEM),
        scratch_shapes=[pltpu.VMEM(x.shape, x.dtype) for x in constants]
        + [
            pltpu.VMEM((2, all_channels, step, LANES), f32),
            pltpu.VMEM((all_channels, step, LANES), f32),
            pltpu.VMEM((shards, copies, step, LANES), f32),
            pltpu.VMEM((shards, tiles, LANES), f32),
            pltpu.VMEM((copies, channels, step, LANES), f32),
            pltpu.VMEM((shards, tiles, LANES), f32),
            pltpu.VMEM((channels, tiles, LANES), f32),
            pltpu.VMEM((1, channels), f32),
            pltpu.SemaphoreType.DMA((2,)),
            pltpu.SemaphoreType.DMA((6,)),
        ]
        + [pltpu.SemaphoreType.DMA] * 8,
        compiler_params=pltpu.CompilerParams(collective_id=0, has_side_effects=True),
    )(
        projected.reshape(3, all_channels, step, LANES),
        filter_taps.reshape(channels, tiles, LANES),
        skip_gain.reshape(1, channels),
        *constants,
    )
    return result.reshape(channels, 1, length)


def solution(mesh):
    return jax.shard_map(
        functools.partial(on_device, mesh.shape["seq"], mesh.shape["ch"]),
        mesh=mesh,
        in_specs=(P(None, None, "seq", "ch"), P("ch", "seq", None), P("ch")),
        out_specs=P("ch", "seq", None),
        check_vma=False,
    )
```

time: 188 us -> 25.2 us (0.13)
  waiting for transfers between devices: 146 us -> 0 us
  Pallas kernels: 0 us -> 23.5 us
  starting transfers between devices: 17.4 us -> 0 us
  matrix products: 9.85 us -> 0 us
  other arithmetic: 7.85 us -> 0 us
  local copies, waits for them, and re-layouts: 5.68 us -> 1.57 us
    ppermute x8 -> x0, waiting for transfers between devices: 139 us -> none  [partner_2(): return lax.ppermute(value, axis, pairs)]
    pallas_call x0 -> x1, Pallas kernels: none -> 23.5 us  [on_device(): pl.pallas_call(functools.partial(kernel, shards, copies, channels, tiles)...]
    ppermute x8 -> x0, starting transfers between devices: 13 us -> none  [partner_2(): return lax.ppermute(value, axis, pairs)]
    dot_general x16 -> x0, matrix products: 9.85 us -> none  [the longest x4 2.47 us: complex_einsum(): product(form, blocks[1], cosine)]
    all_to_all x1 -> x0, waiting for transfers between devices: 6.84 us -> none  [on_device(): lax.all_to_all(projected, 'ch', split_axis=1, concat_axis=3, tiled=True)]
    all_to_all x1 -> x0, starting transfers between devices: 4.39 us -> none  [on_device(): lax.all_to_all(projected, 'ch', split_axis=1, concat_axis=3, tiled=True)]
    select_n x8 -> x0, other arithmetic: 3.98 us -> none  [the longest x4 3.35 us: swaps_forward(): blocks = jnp.where(is_upper, upper_value, blocks + partner)]
    sub x18 -> x0, other arithmetic: 3.01 us -> none  [the longest x4 1.89 us: swaps_forward(): upper_value = rotate(partner - blocks, cosine, sine_part)]
  transfers between devices with their start and end apart: 9 -> 0, of which waited for: 9 -> 0; matrix products, arithmetic and copies ran while one was open for 1% -> 0% of each run, Pallas kernels for 0% -> 0%
where the time goes in v1:
time: 25.2 us; the launch traced here: 25 us
  Pallas kernels  23.5 us (93%)
  local copies, waits for them, and re-layouts  1.57 us (6%)
    pallas_call x1, Pallas kernels, on_device(): pl.pallas_call(functools.partial(kernel, shards, copies, channels, tiles)...  23.5 us
    unnamed x1, local copies, waits for them, and re-layouts  1.57 us

profile of v1, /device:TPU:0, one launch (start us, length us, event | category | flops | bytes accessed | tf_op | source)
XLA Modules:
  0.0 25.0 jit_solution(7156397833957783461)
XLA Ops:
  0.0 23.5 %shard_map.91 = f32[16,16,128]{2,1,0:T(8,128)} custom-call(f32[3,32,8,128]{3,2,1,0:T(8,128)} %bitcast.5, f32[16,16,128]{2,1,0:T(8,128)} %bitcast.6, f32[1,16]{1,0:T(1,128)} %bitcast.7, bf16[2,512,256]{2,1,0:T(8,128)(2,1)} %constant.12.clone.rest_0_, bf16[2,256,512]{2,1,0:T(8,128)(2,1)} %constant.13.clone.rest_1_, ...), custom_call_target="tpu_custom_call" | custom-call | tf_op jit(solution)/shard_map/pallas_call | solution.py:333
  23.5 1.6 %copy.12 = f32[16,1,2048]{2,1,0:T(1,128)} copy(f32[16,1,2048]{2,1,0:T(1,128)} %bitcast.4) | data formatting | bytes 262144

commit v2 on v1

--- a/solution.py
+++ b/solution.py
@@ -87,20 +87,16 @@
     return dot(high, table[0]) + (dot(low, table[0]) + dot(high, table[1]))
 
 
-def convolve(gated, taps, shards, tiles, first, last, lane, shard, turn_one, turn_two):
+def forward(signal, shards, tiles, first, lane, shard, turn_one, turn_two):
     per_group = ROWS // tiles
     groups = shards // per_group
     rows = tiles * shards
-    stages = []
-    for g in range(groups):
-        chosen = slice(g * ROWS, (g + 1) * ROWS)
-        both = jnp.concatenate([gated[chosen], taps[chosen]], axis=1)
-        stages.append(from_left(first, both))
-
-    def rows_of(part, signal):
-        pieces = [
-            s[part * ROWS : (part + 1) * ROWS, signal * LANES : (signal + 1) * LANES] for s in stages
-        ]
+    stages = [
+        from_left_narrow(first, signal[g * ROWS : (g + 1) * ROWS]) for g in range(groups)
+    ]
+
+    def rows_of(part):
+        pieces = [s[part * ROWS : (part + 1) * ROWS] for s in stages]
         if groups == 1:
             return pieces[0]
         pieces = [x.reshape(tiles, per_group, LANES) for x in pieces]
@@ -108,31 +104,35 @@
 
     one_re, one_im = turn_one[0], turn_one[1]
     two_re, two_im = turn_two[0], turn_two[1]
-    spectra = []
-    for signal in range(2):
-        re, im = rows_of(0, signal), rows_of(1, signal)
-        turned = jnp.concatenate([re * one_re - im * one_im, re * one_im + im * one_re], axis=1)
-        spectra.append(from_right(turned, lane))
-    backs = []
-    for q in range(rows // LANES):
-        chosen = slice(q * LANES, (q + 1) * LANES)
+    re, im = rows_of(0), rows_of(1)
+    turned = jnp.concatenate([re * one_re - im * one_im, re * one_im + im * one_re], axis=1)
+    spectrum = from_right(turned, lane)
+    results = []
+    for q in range(0, rows // LANES, 2):
         res, ims = [], []
-        for signal in range(2):
-            re, im = spectra[signal][chosen, :LANES], spectra[signal][chosen, LANES:]
+        for half in range(2):
+            chosen = slice((q + half) * LANES, (q + half + 1) * LANES)
+            re, im = spectrum[chosen, :LANES], spectrum[chosen, LANES:]
             res.append(re * two_re - im * two_im)
             ims.append(re * two_im + im * two_re)
         stacked = jnp.concatenate(
             [jnp.concatenate(res, axis=1), jnp.concatenate(ims, axis=1)], axis=0
         )
-        full = from_left(shard, stacked)
-        g_re, h_re = full[:LANES, :LANES], full[:LANES, LANES:]
-        g_im, h_im = full[LANES:, :LANES], full[LANES:, LANES:]
+        results.append(from_left(shard, stacked))
+    return results
+
+
+def backward(left, right, shards, tiles, lane, shard, turn_one, turn_two):
+    per_group = ROWS // tiles
+    groups = shards // per_group
+    one_re, one_im = turn_one[0], turn_one[1]
+    two_re, two_im = turn_two[0], turn_two[1]
+    turned = []
+    for g, h in zip(left, right):
+        g_re, g_im, h_re, h_im = g[:LANES], g[LANES:], h[:LANES], h[LANES:]
         y_re = g_re * h_re - g_im * h_im
         y_im = g_re * h_im + g_im * h_re
-        backs.append(jnp.concatenate([y_im, y_re], axis=0))
-    turned = []
-    for q in range(0, len(backs), 2):
-        back = from_left(shard, jnp.concatenate(backs[q : q + 2], axis=1))
+        back = from_left(shard, jnp.concatenate([y_im, y_re], axis=0))
         for half in range(2):
             columns = slice(half * LANES, (half + 1) * LANES)
             re, im = back[LANES:, columns], back[:LANES, columns]
@@ -141,23 +141,21 @@
             )
     back = from_right(jnp.concatenate(turned, axis=0), lane)
     re, im = back[:, LANES:], back[:, :LANES]
-    out_re = re * one_re + im * one_im
-    out_im = im * one_re - re * one_im
-    results = []
-    for g in range(groups):
-        if groups == 1:
-            stacked = jnp.concatenate([out_re, out_im], axis=0)
-        else:
-            part = slice(g * per_group, (g + 1) * per_group)
-            stacked = jnp.concatenate(
-                [
-                    x.reshape(tiles, shards, LANES)[:, part].reshape(ROWS, LANES)
-                    for x in (out_re, out_im)
-                ],
-                axis=0,
-            )
-        results.append(from_left_narrow(last, stacked))
-    return results[0] if groups == 1 else jnp.concatenate(results, axis=0)
+    parts = (re * one_re + im * one_im, im * one_re - re * one_im)
+    if groups == 1:
+        return [jnp.concatenate(parts, axis=0)]
+    return [
+        jnp.concatenate(
+            [
+                x.reshape(tiles, shards, LANES)[:, g * per_group : (g + 1) * per_group].reshape(
+                    ROWS, LANES
+                )
+                for x in parts
+            ],
+            axis=0,
+        )
+        for g in range(groups)
+    ]
 
 
 def far_first(count):
@@ -271,20 +269,22 @@
         x.wait()
 
     def transform():
+        first, last, lane, shard, turn_one, turn_two = held
         pltpu.make_async_copy(h_in, h_in, h_recv).wait()
-        pltpu.make_async_copy(g_in, g_in, g_recv).wait()
         slab = gain_in[...]
         column = lax.broadcasted_iota(jnp.int32, slab.shape, 1)
         direct = jnp.sum(jnp.where(column == own_slot, slab, 0.0))
-        signal = g_in[...].reshape(shards * tiles, LANES)
         filt = h_in[...].reshape(shards * tiles, LANES)
         row = lax.broadcasted_iota(jnp.int32, filt.shape, 0)
         column = lax.broadcasted_iota(jnp.int32, filt.shape, 1)
         filt = filt + jnp.where((row == 0) & (column == 0), direct, 0.0)
-        result = convolve(signal, filt, shards, tiles, *held)
-        conv[...] = result.reshape(shards, tiles, LANES)
-        for d in far_first(shards):
-            target = (me + d) % shards
+        right = forward(filt, shards, tiles, first, lane, shard, turn_one, turn_two)
+        pltpu.make_async_copy(g_in, g_in, g_recv).wait()
+        signal = g_in[...].reshape(shards * tiles, LANES)
+        left = forward(signal, shards, tiles, first, lane, shard, turn_one, turn_two)
+        stacks = backward(left, right, shards, tiles, lane, shard, turn_one, turn_two)
+
+        def send_result(target):
             pltpu.make_async_remote_copy(
                 src_ref=conv.at[target],
                 dst_ref=y_in.at[own_slot],
@@ -293,6 +293,24 @@
                 device_id={"seq": target, "ch": mine},
                 device_id_type=MESH,
             ).start()
+
+        if len(stacks) == 1:
+            half = shards // 2
+            high, low = parts_of(stacks[0])
+            both = jnp.concatenate([high, low], axis=1)
+            for turn in range(2):
+                base = (me // half + 1 + turn) % 2 * half
+                chosen = pl.ds(pl.multiple_of(base * tiles, half * tiles), half * tiles)
+                wide = dot(last[0, chosen], both)
+                result = wide[:, :LANES] + (wide[:, LANES:] + dot(last[1, chosen], high))
+                conv[pl.ds(base, half)] = result.reshape(half, tiles, LANES)
+                for d in range(turn, half):
+                    send_result(base + (me + d) % half)
+        else:
+            results = [from_left_narrow(last, x) for x in stacks]
+            conv[...] = jnp.concatenate(results, axis=0).reshape(shards, tiles, LANES)
+            for d in far_first(shards):
+                send_result((me + d) % shards)
         pltpu.make_async_copy(conv.at[me], y_in.at[own_slot], y_recv).start()
 
     when_owner(transform)
@@ -332,7 +350,7 @@
     f32 = jnp.float32
     result = pl.pallas_call(
         functools.partial(kernel, shards, copies, channels, tiles),
-        out_shape=jax.ShapeDtypeStruct((channels, tiles, LANES), f32),
+        out_shape=pltpu.VMEM((channels, tiles, LANES), f32),
         in_specs=[any_spec] * 9,
         out_specs=pl.BlockSpec(memory_space=pltpu.VMEM),
         scratch_shapes=[pltpu.VMEM(x.shape, x.dtype) for x in constants]

time: 25.2 us -> 22.7 us (0.901)
  Pallas kernels: 23.5 us -> 21.9 us
  local copies, waits for them, and re-layouts: 1.57 us -> 0.66 us
    pallas_call x1, Pallas kernels: 23.5 us -> 21.9 us  [on_device(): pl.pallas_call(functools.partial(kernel, shards, copies, channels, tiles)...]
    unnamed x1, local copies, waits for them, and re-layouts: 1.57 us -> 0.66 us
where the time goes in v2:
time: 22.7 us; the launch traced here: 22.5 us
  Pallas kernels  21.9 us (96%)
  local copies, waits for them, and re-layouts  0.66 us (3%)
    pallas_call x1, Pallas kernels, on_device(): pl.pallas_call(functools.partial(kernel, shards, copies, channels, tiles)...  21.9 us
    unnamed x1, local copies, waits for them, and re-layouts  0.66 us

profile of v2, /device:TPU:0, one launch (start us, length us, event | category | flops | bytes accessed | tf_op | source)
XLA Modules:
  0.0 22.5 jit_solution(11888497223313241358)
XLA Ops:
  0.0 21.9 %shard_map.91 = f32[16,16,128]{2,1,0:T(8,128)S(1)} custom-call(f32[3,32,8,128]{3,2,1,0:T(8,128)} %bitcast.5, f32[16,16,128]{2,1,0:T(8,128)} %bitcast.6, f32[1,16]{1,0:T(1,128)} %bitcast.7, bf16[2,512,256]{2,1,0:T(8,128)(2,1)} %constant.12.clone.rest_0_, bf16[2,256,512]{2,1,0:T(8,128)(2,1)} %constant.13.clone.rest_1_, ...), custom_call_target="tpu_custom_call" | custom-call | tf_op jit(solution)/shard_map/pallas_call | solution.py:351
  21.9 0.7 %copy.12 = f32[16,1,2048]{2,1,0:T(1,128)} copy(f32[16,1,2048]{2,1,0:T(1,128)S(1)} %bitcast.4) | data formatting | bytes 262144
